TPU v7x, 32 devices: a whole 2x2x4 slice. The times are simulated.
32 devices in a mesh: groups: 2 (over y), role: 4 (over x, core), tp: 4 (over z).
Axes of the slice: x: 2, y: 2, z: 4, core: 2. Of those that a mesh axis runs over, the one named last changes fastest.
Arguments:
- residual: bfloat16 [64, 8192], P(('groups', 'tp'), 'role'), parts along dimension 0, may hold values from -20 to 20
- attn_gain: float32 [8192], P('role'), may hold values from 0.1 to 1.9
- w_query: bfloat16 [8192, 4096], P('role', 'tp'), may hold values from -0.0625 to 0.0625
- w_key: bfloat16 [8192, 512], P('role', 'tp'), may hold values from -0.0625 to 0.0625
- w_value: bfloat16 [8192, 512], P('role', 'tp'), may hold values from -0.0625 to 0.0625
- w_output: bfloat16 [4096, 8192], P('tp', 'role'), may hold values from -0.09375 to 0.09375
- cache_keys: bfloat16 [64, 256, 512], P(('groups', 'role', 'tp')), parts along dimension 0, may hold values from -300 to 300
- cache_values: bfloat16 [64, 256, 512], P(('groups', 'role', 'tp')), parts along dimension 0, may hold values from -12 to 12
- lengths: int32 [64], P(('groups', 'role', 'tp')), parts along dimension 0, may hold values from 2 to 256
- served: int32 [64], P('groups'), parts along dimension 0, may hold values 0 or 1
- ffn_gain: float32 [8192], P('role'), may hold values from 0.1 to 1.9
- w_gate: bfloat16 [8192, 14336], P('role', 'tp'), may hold values from -0.0625 to 0.0625
- w_up: bfloat16 [8192, 14336], P('role', 'tp'), may hold values from -0.0625 to 0.0625
- w_down: bfloat16 [14336, 8192], P('tp', 'role'), may hold values from -0.046875 to 0.046875
Outputs:
- layer_out: bfloat16 [64, 8192], P(('groups', 'tp'), 'role'), parts along dimension 0
There are 2 independent parts, one for each index of `groups`. A program takes and returns all parts, laid end to end along the dimension named above; an argument that names none is the same for every part. Nothing has to cross between parts.
Inputs may be any that keep to these rules, and one draw needn't show every extreme that they name: Each request's new token stands at position lengths; cached positions from lengths on are unused.
All inputs are finite; a program needn't handle non-finite values.
Results may differ from a plain program's by a relative error of at most 0.024.
Values may be sent and summed in bfloat16 or wider, within the bound.
No kernel may reach another device: no remote copies, remote signals or barrier semaphores. Data moves between devices by JAX's collectives and lax.ppermute only.
A program may use at most 128 MiB of HBM per device.

v0:
```python
import jax
import jax.numpy as jnp
from jax import lax
from jax.sharding import PartitionSpec as P

D = 8192
HEADS = 32
KV_HEADS = 4
HEAD_DIM = 128
WINDOW = 256
GROUP = 8
epsilon = 1e-05
rope_base = 500000.0


def rotate(vectors, positions):
    halfway = vectors.shape[-1] // 2
    frequency = jnp.power(
        jnp.float32(rope_base), -jnp.arange(halfway, dtype=jnp.float32) * 2.0 / vectors.shape[-1]
    )
    angles = positions.astype(jnp.float32)[:, None, None] * frequency[None, None, :]
    cosine = jnp.cos(angles)
    sine_part = jnp.sin(angles)
    leading = vectors[..., :halfway]
    trailing = vectors[..., halfway:]
    return jnp.concatenate(
        [leading * cosine - trailing * sine_part, trailing * cosine + leading * sine_part], axis=-1
    )


def attend(queries, new_key, new_value, keys, values, lengths):
    batch_rows = queries.shape[0]
    factor = HEAD_DIM ** (-0.5)
    grouped = queries.reshape(batch_rows, KV_HEADS, GROUP, HEAD_DIM)
    key_blocks = keys.reshape(batch_rows, WINDOW, KV_HEADS, HEAD_DIM)
    value_blocks = values.reshape(batch_rows, WINDOW, KV_HEADS, HEAD_DIM)
    scores = (
        jnp.einsum("nkgd,nwkd->nkgw", grouped, key_blocks, preferred_element_type=jnp.float32)
        * factor
    )
    self_score = (
        jnp.einsum("nkgd,nkd->nkg", grouped, new_key, preferred_element_type=jnp.float32) * factor
    )
    usable = jnp.arange(WINDOW, dtype=jnp.int32)[None, :] < lengths[:, None]
    scores = jnp.where(usable[:, None, None, :], scores, -jnp.inf)
    highest = jnp.maximum(jnp.max(scores, axis=-1), self_score)
    weights = jnp.exp(scores - highest[..., None])
    self_weight = jnp.exp(self_score - highest)
    denominator = jnp.sum(weights, axis=-1) + self_weight
    chances = (weights / denominator[..., None]).astype(jnp.bfloat16)
    self_chance = (self_weight / denominator).astype(jnp.bfloat16)
    attended = jnp.einsum(
        "nkgw,nwkd->nkgd", chances, value_blocks, preferred_element_type=jnp.float32
    )
    attended = (
        attended
        + self_chance.astype(jnp.float32)[..., None] * new_value.astype(jnp.float32)[:, :, None, :]
    )
    return attended.reshape(batch_rows, HEADS * HEAD_DIM).astype(jnp.bfloat16)


def feed_forward(middle, ffn_gain, w_gate, w_up, w_down):
    widened = middle.astype(jnp.float32)
    squares = lax.psum(jnp.sum(widened * widened, axis=1), "role")
    inverse = lax.rsqrt(squares / D + epsilon)
    mid_normed = (widened * inverse[:, None] * ffn_gain[None, :]).astype(jnp.bfloat16)
    gate_part = jnp.dot(mid_normed, w_gate, preferred_element_type=jnp.float32)
    up_part = jnp.dot(mid_normed, w_up, preferred_element_type=jnp.float32)
    gate_total, up_total = (
        lax.psum(gate_part.astype(jnp.bfloat16), "role").astype(jnp.float32),
        lax.psum(up_part.astype(jnp.bfloat16), "role").astype(jnp.float32),
    )
    hidden = (jax.nn.silu(gate_total) * up_total).astype(jnp.bfloat16)
    down_terms = jnp.dot(hidden, w_down, preferred_element_type=jnp.float32)
    return lax.psum_scatter(
        down_terms.astype(jnp.bfloat16), "tp", scatter_dimension=0, tiled=True
    ).astype(jnp.float32)


def local(
    residual,
    attn_gain,
    w_query,
    w_key,
    w_value,
    w_output,
    cache_keys,
    cache_values,
    lengths,
    served,
    ffn_gain,
    w_gate,
    w_up,
    w_down,
):
    own_rows = residual.shape[0]
    tp_count = lax.axis_size("tp")
    row_start = lax.axis_index("tp") * own_rows
    live_own = lax.dynamic_slice_in_dim(served, row_start, own_rows, 0).astype(jnp.float32)[:, None]
    rows_all = lax.all_gather(residual, "tp", axis=0, tiled=True)
    widened = rows_all.astype(jnp.float32)
    squares = lax.psum(jnp.sum(widened * widened, axis=1), "role")
    inverse = lax.rsqrt(squares / D + epsilon)
    normed = (widened * inverse[:, None] * attn_gain[None, :]).astype(jnp.bfloat16)
    partial_value = jnp.concatenate(
        [
            jnp.dot(normed, w_query, preferred_element_type=jnp.float32),
            jnp.dot(normed, w_key, preferred_element_type=jnp.float32),
            jnp.dot(normed, w_value, preferred_element_type=jnp.float32),
        ],
        axis=1,
    )
    summed = lax.psum_scatter(
        partial_value.astype(jnp.bfloat16), "role", scatter_dimension=0, tiled=True
    ).astype(jnp.float32)
    gathered = lax.all_to_all(
        summed.astype(jnp.bfloat16), "tp", split_axis=0, concat_axis=1, tiled=True
    ).astype(summed.dtype)
    local_rows = gathered.shape[0]
    query_cols = w_query.shape[1]
    kv_cols = w_key.shape[1]
    blocks = gathered.reshape(local_rows, tp_count, query_cols + 2 * kv_cols)
    queries = blocks[:, :, :query_cols].reshape(local_rows, HEADS, HEAD_DIM)
    new_key = blocks[:, :, query_cols : query_cols + kv_cols].reshape(
        local_rows, KV_HEADS, HEAD_DIM
    )
    new_value = (
        blocks[:, :, query_cols + kv_cols :]
        .reshape(local_rows, KV_HEADS, HEAD_DIM)
        .astype(jnp.bfloat16)
    )
    queries = rotate(queries, lengths).astype(jnp.bfloat16)
    new_key = rotate(new_key, lengths).astype(jnp.bfloat16)
    attended = attend(queries, new_key, new_value, cache_keys, cache_values, lengths)
    head_block = lax.all_to_all(attended, "tp", split_axis=1, concat_axis=0, tiled=True)
    attn_terms = jnp.dot(
        lax.all_gather(head_block, "role", axis=0, tiled=True),
        w_output,
        preferred_element_type=jnp.float32,
    )
    attn = lax.psum_scatter(
        attn_terms.astype(jnp.bfloat16), "tp", scatter_dimension=0, tiled=True
    ).astype(jnp.float32)
    middle_own = (residual.astype(jnp.float32) + live_own * attn).astype(jnp.bfloat16)
    middle = lax.all_gather(middle_own, "tp", axis=0, tiled=True)
    ffn = feed_forward(middle, ffn_gain, w_gate, w_up, w_down)
    return (middle_own.astype(jnp.float32) + live_own * ffn).astype(jnp.bfloat16)


def solution(mesh):
    return jax.shard_map(
        local,
        mesh=mesh,
        in_specs=(
            P(("groups", "tp"), "role"),
            P("role"),
            P("role", "tp"),
            P("role", "tp"),
            P("role", "tp"),
            P("tp", "role"),
            P(("groups", "role", "tp"), None, None),
            P(("groups", "role", "tp"), None, None),
            P(("groups", "role", "tp")),
            P("groups"),
            P("role"),
            P("role", "tp"),
            P("role", "tp"),
            P("tp", "role"),
        ),
        out_specs=P(("groups", "tp"), "role"),
        check_vma=False,
    )
```

profile of v0, /device:TPU:0, one launch (start us, length us, event | category | flops | bytes accessed | tf_op | source)
XLA Modules:
  0.0 208.5 jit_solution(7875377142544412740)
XLA Ops:
  6.5 15.4 %all_gather.9 = bf16[32,2048]{1,0:T(8,128)(2,1)S(1)} all-gather(bf16[8,2048]{1,0:T(8,128)(2,1)} %param.14), channel_id=1, replica_groups=mesh['groups'=2,'role'=4,'tp'=4] {'tp'}, dimensions={0}, use_global_device_ids=true | all-gather | bytes 163840 | tf_op jit(solution)/shard_map/all_gather | solution.py:100
  22.0 0.1 fusion.11
  22.1 5.7 %psum.28 = f32[32]{0:T(128)S(1)} all-reduce(f32[32]{0:T(128)S(1)} %fusion.11), channel_id=1, replica_groups=mesh['groups'=2,'role'=4,'tp'=4] {'role'}, use_global_device_ids=true, to_apply=%region_1.0 | all-reduce | flops 32 | bytes 256 | tf_op jit(solution)/shard_map/psum | solution.py:102
  27.8 1.3 convolution_convert_fusion.6
  29.1 1.3 convolution_convert_fusion.5
  30.4 3.1 %convolution_convert_fusion.4 = bf16[32,1024]{1,0:T(8,128)(2,1)S(1)} fusion(bf16[2048,1024]{1,0:T(8,128)(2,1)} %param.16, bf16[32,2048]{1,0:T(8,128)(2,1)S(1)} %all_gather.9, f32[2048]{0:T(1024)} %param.15, f32[32]{0:T(128)S(1)} %add_rsqrt_fusion.1), kind=kOutput, calls=%fused_computation.4 | convolution fusion | flops 134512640 | bytes 4399232 | tf_op jit(solution)/shard_map/dot_general | solution.py:107
  33.5 0.6 pad_maximum_fusion
  34.2 0.7 convert_element_type.97
  35.0 20.6 %reduce-scatter.4.cloned.1.call-done = bf16[8,1280]{1,0:T(8,128)(2,1)} async-done(((bf16[32,1280]{1,0:T(8,128)(2,1)}), bf16[8,1280]{1,0:T(8,128)(2,1)}) %reduce-scatter.4.cloned.1.call-update) | async-done | bytes 20496 | tf_op jit(solution)/shard_map/reduce_scatter | solution.py:113
  55.5 1.3 all_to_all.22
  56.9 4.6 %all-to-all-start = ((bf16[4,2,1280]{2,1,0:T(2,128)(2,1)}), bf16[4,2,1280]{2,1,0:T(2,128)(2,1)S(1)}, u32[]{:S(2)}, u32[]{:S(2)}) async-start(bf16[4,2,1280]{2,1,0:T(2,128)(2,1)} %all_to_all.22), calls=%async_computation.1 | async-start | bytes 40960 | tf_op jit(solution)/shard_map/all_to_all | solution.py:116
  61.5 0.7 iota_compare_fusion
  62.2 4.9 %all-to-all-done = bf16[4,2,1280]{2,1,0:T(2,128)(2,1)S(1)} async-done(((bf16[4,2,1280]{2,1,0:T(2,128)(2,1)}), bf16[4,2,1280]{2,1,0:T(2,128)(2,1)S(1)}, u32[]{:S(2)}, u32[]{:S(2)}) %all-to-all-start) | async-done | bytes 20512 | tf_op jit(solution)/shard_map/all_to_all | solution.py:116
  67.4 0.2 fusion.26
  67.6 0.3 fusion.37
  67.9 0.2 fusion.19
  68.2 1.3 fusion.1
  69.5 8.0 %all_to_all.29 = bf16[2,4,1024]{2,0,1:T(2,128)(2,1)S(1)} all-to-all(bf16[2,4,1024]{2,0,1:T(2,128)(2,1)S(1)} %copy.30), channel_id=1, replica_groups=mesh['groups'=2,'role'=4,'tp'=4] {'tp'}, dimensions={1} | all-to-all | bytes 32768 | tf_op jit(solution)/shard_map/all_to_all | solution.py:135
  77.5 5.2 %all_gather.10 = bf16[32,1024]{1,0:T(8,128)(2,1)S(1)} all-gather(bf16[8,1024]{1,0:T(8,128)(2,1)S(1)} %all_to_all.26), channel_id=1, replica_groups=mesh['groups'=2,'role'=4,'tp'=4] {'role'}, dimensions={0}, use_global_device_ids=true | all-gather | bytes 81920 | tf_op jit(solution)/shard_map/all_gather | solution.py:137
  82.7 3.7 %convolution_convert_fusion.3 = bf16[32,2048]{1,0:T(8,128)(2,1)} fusion(bf16[32,1024]{1,0:T(8,128)(2,1)S(1)} %all_gather.10, bf16[1024,2048]{1,0:T(8,128)(2,1)} %param.19), kind=kOutput, calls=%fused_computation.3 | convolution fusion | flops 134283264 | bytes 4390912 | tf_op jit(solution)/shard_map/dot_general | solution.py:136
  86.4 0.7 dynamic-slice_convert_fusion
  87.2 16.1 %reduce-scatter.6.cloned.1.call-done = bf16[8,2048]{1,0:T(8,128)(2,1)} async-done(((bf16[32,2048]{1,0:T(8,128)(2,1)}), bf16[8,2048]{1,0:T(8,128)(2,1)}) %reduce-scatter.6.cloned.1.call-update) | async-done | bytes 32784 | tf_op jit(solution)/shard_map/reduce_scatter | solution.py:141
  103.3 0.8 add_convert_fusion.1
  104.2 13.4 %all_gather.11 = bf16[32,2048]{1,0:T(8,128)(2,1)S(1)} all-gather(bf16[8,2048]{1,0:T(8,128)(2,1)S(1)} %add_convert_fusion.1), channel_id=1, replica_groups=mesh['groups'=2,'role'=4,'tp'=4] {'tp'}, dimensions={0}, use_global_device_ids=true | all-gather | bytes 163840 | tf_op jit(solution)/shard_map/all_gather | solution.py:145
  117.5 0.1 fusion.14
  117.7 5.7 %psum.29 = f32[32]{0:T(128)S(1)} all-reduce(f32[32]{0:T(128)S(1)} %fusion.14), channel_id=1, replica_groups=mesh['groups'=2,'role'=4,'tp'=4] {'role'}, use_global_device_ids=true, to_apply=%region_7.8 | all-reduce | flops 32 | bytes 256 | tf_op jit(solution)/shard_map/psum | solution.py:64
  123.3 8.5 %convolution_convert_fusion = bf16[32,3584]{1,0:T(8,128)(2,1)} fusion(bf16[2048,3584]{1,0:T(8,128)(2,1)} %param.26, bf16[32,2048]{1,0:T(8,128)(2,1)S(1)} %all_gather.11, f32[2048]{0:T(1024)} %param.24, f32[32]{0:T(128)S(1)} %add_rsqrt_fusion), kind=kOutput, calls=%fused_computation | convolution fusion | flops 470138880 | bytes 15048832 | tf_op jit(solution)/shard_map/dot_general | solution.py:68
  131.9 8.5 %convolution_convert_fusion.1 = bf16[32,3584]{1,0:T(8,128)(2,1)} fusion(bf16[2048,3584]{1,0:T(8,128)(2,1)} %param.25, bf16[32,2048]{1,0:T(8,128)(2,1)S(1)} %all_gather.11, f32[2048]{0:T(1024)S(1)} %copy-done.1, f32[32]{0:T(128)S(1)} %add_rsqrt_fusion), kind=kOutput, calls=%fused_computation.1 | convolution fusion | flops 470138880 | bytes 15048832 | tf_op jit(solution)/shard_map/dot_general | solution.py:67
  140.5 31.7 %all-reduce.3.cloned.1.call-done = (bf16[32,3584]{1,0:T(8,128)(2,1)}, bf16[32,3584]{1,0:T(8,128)(2,1)}) async-done(((bf16[32,3584]{1,0:T(8,128)(2,1)}, bf16[32,3584]{1,0:T(8,128)(2,1)}), (bf16[32,3584]{1,0:T(8,128)(2,1)}, bf16[32,3584]{1,0:T(8,128)(2,1)})) %all-reduce.3.cloned.1.call-update) | async-done | bytes 458768 | tf_op jit(solution)/shard_map/psum | solution.py:71
  172.2 8.7 %convolution_convert_fusion.2 = bf16[32,2048]{1,0:T(8,128)(2,1)} fusion(bf16[3584,2048]{1,0:T(8,128)(2,1)} %param.27, bf16[32,3584]{1,0:T(8,128)(2,1)} %get-tuple-element.5, bf16[32,3584]{1,0:T(8,128)(2,1)} %get-tuple-element.6), kind=kOutput, calls=%fused_computation.2 | convolution fusion | flops 470745088 | bytes 15269888 | tf_op jit(solution)/shard_map/dot_general | solution.py:74
  180.9 19.6 %reduce-scatter.8.cloned.1.call-done = bf16[8,2048]{1,0:T(8,128)(2,1)} async-done(((bf16[32,2048]{1,0:T(8,128)(2,1)}), bf16[8,2048]{1,0:T(8,128)(2,1)}) %reduce-scatter.8.cloned.1.call-update) | async-done | bytes 32784 | tf_op jit(solution)/shard_map/reduce_scatter | solution.py:75
  200.5 1.4 add_convert_fusion
  (28 shorter events, 0.6 us)
Async XLA Ops:
  6.5 61.1 %copy-start = (bf16[2,256,512]{2,1,0:T(8,128)(2,1)S(1)}, bf16[2,256,512]{2,1,0:T(8,128)(2,1)}, u32[]{:S(2)}) copy-start(bf16[2,256,512]{2,1,0:T(8,128)(2,1)} %param.20) | copy-start | bytes 1572868
  6.5 49.0 %reduce-scatter.4.cloned.1.call-start = ((), (), s32[]{:S(2)}) async-start(), calls=%async_computation.5 | async-start | bytes 102400 | tf_op jit(solution)/shard_map/reduce_scatter | solution.py:113
  56.9 10.2 %all-to-all-start = ((bf16[4,2,1280]{2,1,0:T(2,128)(2,1)}), bf16[4,2,1280]{2,1,0:T(2,128)(2,1)S(1)}, u32[]{:S(2)}, u32[]{:S(2)}) async-start(bf16[4,2,1280]{2,1,0:T(2,128)(2,1)} %all_to_all.22), calls=%async_computation.1 | async-start | bytes 40960 | tf_op jit(solution)/shard_map/all_to_all | solution.py:116
  61.5 41.9 %reduce-scatter.6.cloned.1.call-start = ((), (), s32[]{:S(2)}) async-start(), calls=%async_computation.6 | async-start | bytes 163840 | tf_op jit(solution)/shard_map/reduce_scatter | solution.py:141
  67.2 64.6 %copy-start.1 = (f32[2048]{0:T(1024)S(1)}, f32[2048]{0:T(1024)}, u32[]{:S(2)}) copy-start(f32[2048]{0:T(1024)} %param.24) | copy-start | bytes 24580
  86.4 85.8 %all-reduce.3.cloned.1.call-start = ((), (), s32[]{:S(2)}) async-start(), calls=%async_computation.8 | async-start | bytes 917504 | tf_op jit(solution)/shard_map/psum | solution.py:71
  140.4 60.1 %reduce-scatter.8.cloned.1.call-start = ((), (), s32[]{:S(2)}) async-start(), calls=%async_computation.7 | async-start | bytes 163840 | tf_op jit(solution)/shard_map/reduce_scatter | solution.py:75
Sparse Core Ops, SparseCore 0:
  34.3 21.1 reduce-scatter.3
  86.5 16.7 reduce-scatter.5
  140.5 31.5 all-reduce.2
  181.0 19.4 reduce-scatter.7
where the time goes:
time: 209 us
  waiting for transfers between devices  93 us (44%)
  blocking collectives  53.3 us (26%)
  matrix products  37 us (18%)
  between operations  13.2 us (6%)
  other arithmetic  5.94 us (3%)
  starting transfers between devices  4.69 us (2%)
    psum x1, waiting for transfers between devices, feed_forward(): lax.psum(up_part.astype(jnp.bfloat16), 'role').astype(jnp.float32)  31.7 us
    reduce_scatter x1, waiting for transfers between devices, local(): lax.psum_scatter(partial_value.astype(jnp.bfloat16), 'role', scatter_dime...  20.6 us
    reduce_scatter x1, waiting for transfers between devices, feed_forward(): lax.psum_scatter(down_terms.astype(jnp.bfloat16), 'tp', scatter_dimension...  19.6 us
    reduce_scatter x1, waiting for transfers between devices, local(): lax.psum_scatter(attn_terms.astype(jnp.bfloat16), 'tp', scatter_dimension...  16.1 us
    all_gather x1, blocking collectives, local(): rows_all = lax.all_gather(residual, 'tp', axis=0, tiled=True)  15.4 us
    all_gather x1, blocking collectives, local(): middle = lax.all_gather(middle_own, 'tp', axis=0, tiled=True)  13.4 us
    dot_general x1, matrix products, feed_forward(): down_terms = jnp.dot(hidden, w_down, preferred_element_type=jnp.float32)  8.7 us
    dot_general x1, matrix products, feed_forward(): gate_part = jnp.dot(mid_normed, w_gate, preferred_element_type=jnp.float32)  8.54 us
  transfers between devices with their start and end apart: 5, of which 5 were waited for; matrix products, arithmetic and copies ran while one was open for 1% of the time, Pallas kernels for 0%

commit v1 on v0

--- a/solution.py
+++ b/solution.py
@@ -11,6 +11,16 @@
 GROUP = 8
 epsilon = 1e-05
 rope_base = 500000.0
+
+
+def pass_along(shard, axis, dim):
+    size = lax.axis_size(axis)
+    moving, blocks = (shard, [shard])
+    for _ in range(size - 1):
+        moving = lax.ppermute(moving, axis, [(i, (i + 1) % size) for i in range(size)])
+        blocks.insert(0, moving)
+    line = jnp.concatenate(blocks, axis=dim)
+    return jnp.roll(line, (lax.axis_index(axis) + 1) * shard.shape[dim], axis=dim)
 
 
 def rotate(vectors, positions):
@@ -142,7 +152,7 @@
         attn_terms.astype(jnp.bfloat16), "tp", scatter_dimension=0, tiled=True
     ).astype(jnp.float32)
     middle_own = (residual.astype(jnp.float32) + live_own * attn).astype(jnp.bfloat16)
-    middle = lax.all_gather(middle_own, "tp", axis=0, tiled=True)
+    middle = pass_along(middle_own, "tp", 0)
     ffn = feed_forward(middle, ffn_gain, w_gate, w_up, w_down)
     return (middle_own.astype(jnp.float32) + live_own * ffn).astype(jnp.bfloat16)
 

time: 209 us -> 213 us (1.019)
  waiting for transfers between devices: 93 us -> 110 us
  blocking collectives: 53.3 us -> 39.9 us
    ppermute x0 -> x3, waiting for transfers between devices: none -> 17.4 us  [pass_along(): lax.ppermute(moving, axis, [(i, (i + 1) % size) for i in range(size)])]
    all_gather x1 -> x0, blocking collectives: 13.4 us -> none  [local(): middle = lax.all_gather(middle_own, 'tp', axis=0, tiled=True)]
  transfers between devices with their start and end apart: 5 -> 8, of which waited for: 5 -> 8; matrix products, arithmetic and copies ran while one was open for 1% -> 1% of each run, Pallas kernels for 0% -> 0%
where the time goes in v1:
time: 213 us
  waiting for transfers between devices  110 us (52%)
  blocking collectives  39.9 us (19%)
  matrix products  37 us (17%)
  between operations  13.3 us (6%)
  other arithmetic  5.95 us (3%)
  starting transfers between devices  4.75 us (2%)
    psum x1, waiting for transfers between devices, feed_forward(): lax.psum(up_part.astype(jnp.bfloat16), 'role').astype(jnp.float32)  31.7 us
    reduce_scatter x1, waiting for transfers between devices, local(): lax.psum_scatter(partial_value.astype(jnp.bfloat16), 'role', scatter_dime...  20.6 us
    reduce_scatter x1, waiting for transfers between devices, feed_forward(): lax.psum_scatter(down_terms.astype(jnp.bfloat16), 'tp', scatter_dimension...  19.6 us
    ppermute x3, waiting for transfers between devices, pass_along(): lax.ppermute(moving, axis, [(i, (i + 1) % size) for i in range(size)])  17.4 us
    reduce_scatter x1, waiting for transfers between devices, local(): lax.psum_scatter(attn_terms.astype(jnp.bfloat16), 'tp', scatter_dimension...  16.2 us
    all_gather x1, blocking collectives, local(): rows_all = lax.all_gather(residual, 'tp', axis=0, tiled=True)  15.4 us
    dot_general x1, matrix products, feed_forward(): down_terms = jnp.dot(hidden, w_down, preferred_element_type=jnp.float32)  8.71 us
    dot_general x1, matrix products, feed_forward(): gate_part = jnp.dot(mid_normed, w_gate, preferred_element_type=jnp.float32)  8.54 us
  transfers between devices with their start and end apart: 8, of which 8 were waited for; matrix products, arithmetic and copies ran while one was open for 1% of the time, Pallas kernels for 0%

profile of v1, /device:TPU:0, one launch (start us, length us, event | category | flops | bytes accessed | tf_op | source)
XLA Modules:
  0.0 212.7 jit_solution(6557733546753841739)
XLA Ops:
  6.5 15.4 %all_gather.6 = bf16[32,2048]{1,0:T(8,128)(2,1)S(1)} all-gather(bf16[8,2048]{1,0:T(8,128)(2,1)} %param.14), channel_id=1, replica_groups=mesh['groups'=2,'role'=4,'tp'=4] {'tp'}, dimensions={0}, use_global_device_ids=true | all-gather | bytes 163840 | tf_op jit(solution)/shard_map/all_gather | solution.py:110
  22.1 5.7 %psum.28 = f32[32]{0:T(128)S(1)} all-reduce(f32[32]{0:T(128)S(1)} %fusion.11), channel_id=1, replica_groups=mesh['groups'=2,'role'=4,'tp'=4] {'role'}, use_global_device_ids=true, to_apply=%region_1.0 | all-reduce | flops 32 | bytes 256 | tf_op jit(solution)/shard_map/psum | solution.py:112
  27.8 1.3 convolution_convert_fusion.6
  29.1 1.3 convolution_convert_fusion.5
  30.4 3.1 %convolution_convert_fusion.4 = bf16[32,1024]{1,0:T(8,128)(2,1)S(1)} fusion(bf16[2048,1024]{1,0:T(8,128)(2,1)} %param.16, bf16[32,2048]{1,0:T(8,128)(2,1)S(1)} %all_gather.6, f32[2048]{0:T(1024)} %param.15, f32[32]{0:T(128)S(1)} %add_rsqrt_fusion.1), kind=kOutput, calls=%fused_computation.4 | convolution fusion | flops 134512640 | bytes 4399232 | tf_op jit(solution)/shard_map/dot_general | solution.py:117
  33.5 0.6 pad_maximum_fusion
  34.2 0.7 convert_element_type.97
  35.0 20.6 %reduce-scatter.4.cloned.1.call-done = bf16[8,1280]{1,0:T(8,128)(2,1)} async-done(((bf16[32,1280]{1,0:T(8,128)(2,1)}), bf16[8,1280]{1,0:T(8,128)(2,1)}) %reduce-scatter.4.cloned.1.call-update) | async-done | bytes 20496 | tf_op jit(solution)/shard_map/reduce_scatter | solution.py:123
  55.5 1.3 all_to_all.22
  56.9 4.6 %all-to-all-start = ((bf16[4,2,1280]{2,1,0:T(2,128)(2,1)}), bf16[4,2,1280]{2,1,0:T(2,128)(2,1)S(1)}, u32[]{:S(2)}, u32[]{:S(2)}) async-start(bf16[4,2,1280]{2,1,0:T(2,128)(2,1)} %all_to_all.22), calls=%async_computation.1 | async-start | bytes 40960 | tf_op jit(solution)/shard_map/all_to_all | solution.py:126
  61.5 0.7 iota_compare_fusion
  62.2 4.9 %all-to-all-done = bf16[4,2,1280]{2,1,0:T(2,128)(2,1)S(1)} async-done(((bf16[4,2,1280]{2,1,0:T(2,128)(2,1)}), bf16[4,2,1280]{2,1,0:T(2,128)(2,1)S(1)}, u32[]{:S(2)}, u32[]{:S(2)}) %all-to-all-start) | async-done | bytes 20512 | tf_op jit(solution)/shard_map/all_to_all | solution.py:126
  67.4 0.2 fusion.26
  67.6 0.3 fusion.39
  67.9 0.2 fusion.19
  68.2 1.3 fusion.1
  69.5 8.0 %all_to_all.29 = bf16[2,4,1024]{2,0,1:T(2,128)(2,1)S(1)} all-to-all(bf16[2,4,1024]{2,0,1:T(2,128)(2,1)S(1)} %copy.30), channel_id=1, replica_groups=mesh['groups'=2,'role'=4,'tp'=4] {'tp'}, dimensions={1} | all-to-all | bytes 32768 | tf_op jit(solution)/shard_map/all_to_all | solution.py:145
  77.5 5.2 %all_gather.7 = bf16[32,1024]{1,0:T(8,128)(2,1)S(1)} all-gather(bf16[8,1024]{1,0:T(8,128)(2,1)S(1)} %all_to_all.26), channel_id=1, replica_groups=mesh['groups'=2,'role'=4,'tp'=4] {'role'}, dimensions={0}, use_global_device_ids=true | all-gather | bytes 81920 | tf_op jit(solution)/shard_map/all_gather | solution.py:147
  82.7 3.7 %convolution_convert_fusion.3 = bf16[32,2048]{1,0:T(8,128)(2,1)} fusion(bf16[32,1024]{1,0:T(8,128)(2,1)S(1)} %all_gather.7, bf16[1024,2048]{1,0:T(8,128)(2,1)} %param.19), kind=kOutput, calls=%fused_computation.3 | convolution fusion | flops 134283264 | bytes 4390912 | tf_op jit(solution)/shard_map/dot_general | solution.py:146
  86.4 0.7 dynamic-slice_convert_fusion
  87.2 16.2 %reduce-scatter.6.cloned.1.call-done = bf16[8,2048]{1,0:T(8,128)(2,1)} async-done(((bf16[32,2048]{1,0:T(8,128)(2,1)}), bf16[8,2048]{1,0:T(8,128)(2,1)}) %reduce-scatter.6.cloned.1.call-update) | async-done | bytes 32784 | tf_op jit(solution)/shard_map/reduce_scatter | solution.py:151
  103.3 0.8 add_convert_fusion.1
  104.2 5.7 %collective-permute-done = bf16[8,2048]{1,0:T(8,128)(2,1)S(1)} collective-permute-done((bf16[8,2048]{1,0:T(8,128)(2,1)S(1)}, bf16[8,2048]{1,0:T(8,128)(2,1)S(1)}, u32[]{:S(2)}, u32[]{:S(2)}) %collective-permute-start) | collective-permute-done | bytes 32800 | tf_op jit(solution)/shard_map/ppermute | solution.py:20
  110.0 6.0 %collective-permute-done.1 = bf16[8,2048]{1,0:T(8,128)(2,1)S(1)} collective-permute-done((bf16[8,2048]{1,0:T(8,128)(2,1)S(1)}, bf16[8,2048]{1,0:T(8,128)(2,1)S(1)}, u32[]{:S(2)}, u32[]{:S(2)}) %collective-permute-start.1) | collective-permute-done | bytes 32800 | tf_op jit(solution)/shard_map/ppermute | solution.py:20
  115.9 5.7 %collective-permute-done.2 = bf16[8,2048]{1,0:T(8,128)(2,1)S(1)} collective-permute-done((bf16[8,2048]{1,0:T(8,128)(2,1)S(1)}, bf16[8,2048]{1,0:T(8,128)(2,1)S(1)}, u32[]{:S(2)}, u32[]{:S(2)}) %collective-permute-start.2) | collective-permute-done | bytes 32800 | tf_op jit(solution)/shard_map/ppermute | solution.py:20
  121.9 5.7 %psum.29 = f32[32]{0:T(128)S(1)} all-reduce(f32[32]{0:T(128)S(1)} %fusion.14), channel_id=1, replica_groups=mesh['groups'=2,'role'=4,'tp'=4] {'role'}, use_global_device_ids=true, to_apply=%region_7.8 | all-reduce | flops 32 | bytes 256 | tf_op jit(solution)/shard_map/psum | solution.py:74
  127.5 8.5 %convolution_convert_fusion = bf16[32,3584]{1,0:T(8,128)(2,1)} fusion(bf16[2048,3584]{1,0:T(8,128)(2,1)} %param.26, f32[2048]{0:T(1024)} %param.24, f32[32]{0:T(128)S(1)} %add_rsqrt_fusion, bf16[64,2048]{1,0:T(8,128)(2,1)S(1)} %constant_dynamic-update-slice_fusion, s32[]{:T(128)S(6)} %select_n.23), kind=kOutput, calls=%fused_computation | convolution fusion | flops 470138880 | bytes 15049220 | tf_op jit(solution)/shard_map/dot_general | solution.py:78
  136.1 8.5 %convolution_convert_fusion.1 = bf16[32,3584]{1,0:T(8,128)(2,1)} fusion(bf16[2048,3584]{1,0:T(8,128)(2,1)} %param.25, f32[2048]{0:T(1024)S(1)} %copy-done.1, f32[32]{0:T(128)S(1)} %add_rsqrt_fusion, bf16[64,2048]{1,0:T(8,128)(2,1)S(1)} %constant_dynamic-update-slice_fusion, s32[]{:T(128)S(6)} %select_n.23), kind=kOutput, calls=%fused_computation.1 | convolution fusion | flops 470138880 | bytes 15049220 | tf_op jit(solution)/shard_map/dot_general | solution.py:77
  144.7 31.7 %all-reduce.3.cloned.1.call-done = (bf16[32,3584]{1,0:T(8,128)(2,1)}, bf16[32,3584]{1,0:T(8,128)(2,1)}) async-done(((bf16[32,3584]{1,0:T(8,128)(2,1)}, bf16[32,3584]{1,0:T(8,128)(2,1)}), (bf16[32,3584]{1,0:T(8,128)(2,1)}, bf16[32,3584]{1,0:T(8,128)(2,1)})) %all-reduce.3.cloned.1.call-update) | async-done | bytes 458768 | tf_op jit(solution)/shard_map/psum | solution.py:81
  176.4 8.7 %convolution_convert_fusion.2 = bf16[32,2048]{1,0:T(8,128)(2,1)} fusion(bf16[3584,2048]{1,0:T(8,128)(2,1)} %param.27, bf16[32,3584]{1,0:T(8,128)(2,1)} %get-tuple-element.5, bf16[32,3584]{1,0:T(8,128)(2,1)} %get-tuple-element.6), kind=kOutput, calls=%fused_computation.2 | convolution fusion | flops 470745088 | bytes 15269888 | tf_op jit(solution)/shard_map/dot_general | solution.py:84
  185.1 19.6 %reduce-scatter.8.cloned.1.call-done = bf16[8,2048]{1,0:T(8,128)(2,1)} async-done(((bf16[32,2048]{1,0:T(8,128)(2,1)}), bf16[8,2048]{1,0:T(8,128)(2,1)}) %reduce-scatter.8.cloned.1.call-update) | async-done | bytes 32784 | tf_op jit(solution)/shard_map/reduce_scatter | solution.py:85
  204.7 1.4 add_convert_fusion
  (41 shorter events, 1.0 us)
Async XLA Ops:
  6.5 61.1 %copy-start = (bf16[2,256,512]{2,1,0:T(8,128)(2,1)S(1)}, bf16[2,256,512]{2,1,0:T(8,128)(2,1)}, u32[]{:S(2)}) copy-start(bf16[2,256,512]{2,1,0:T(8,128)(2,1)} %param.20) | copy-start | bytes 1572868
  6.5 49.0 %reduce-scatter.4.cloned.1.call-start = ((), (), s32[]{:S(2)}) async-start(), calls=%async_computation.5 | async-start | bytes 102400 | tf_op jit(solution)/shard_map/reduce_scatter | solution.py:123
  56.9 10.2 %all-to-all-start = ((bf16[4,2,1280]{2,1,0:T(2,128)(2,1)}), bf16[4,2,1280]{2,1,0:T(2,128)(2,1)S(1)}, u32[]{:S(2)}, u32[]{:S(2)}) async-start(bf16[4,2,1280]{2,1,0:T(2,128)(2,1)} %all_to_all.22), calls=%async_computation.1 | async-start | bytes 40960 | tf_op jit(solution)/shard_map/all_to_all | solution.py:126
  61.5 41.9 %reduce-scatter.6.cloned.1.call-start = ((), (), s32[]{:S(2)}) async-start(), calls=%async_computation.6 | async-start | bytes 163840 | tf_op jit(solution)/shard_map/reduce_scatter | solution.py:151
  67.6 68.5 %copy-start.1 = (f32[2048]{0:T(1024)S(1)}, f32[2048]{0:T(1024)}, u32[]{:S(2)}) copy-start(f32[2048]{0:T(1024)} %param.24) | copy-start | bytes 24580
  86.4 90.0 %all-reduce.3.cloned.1.call-start = ((), (), s32[]{:S(2)}) async-start(), calls=%async_computation.8 | async-start | bytes 917504 | tf_op jit(solution)/shard_map/psum | solution.py:81
  104.2 5.8 %collective-permute-start = (bf16[8,2048]{1,0:T(8,128)(2,1)S(1)}, bf16[8,2048]{1,0:T(8,128)(2,1)S(1)}, u32[]{:S(2)}, u32[]{:S(2)}) collective-permute-start(bf16[8,2048]{1,0:T(8,128)(2,1)S(1)} %add_convert_fusion.1), channel_id=1, source_target_pairs={{0,1},{1,2},{2,3},{3,0},{4,5},{5,6},{6,7},{7,4},{8,9},{9,10},{10,1... | collective-permute-start | bytes 98312 | tf_op jit(solution)/shard_map/ppermute | solution.py:20
  109.9 6.0 %collective-permute-start.1 = (bf16[8,2048]{1,0:T(8,128)(2,1)S(1)}, bf16[8,2048]{1,0:T(8,128)(2,1)S(1)}, u32[]{:S(2)}, u32[]{:S(2)}) collective-permute-start(bf16[8,2048]{1,0:T(8,128)(2,1)S(1)} %collective-permute-done), channel_id=1, source_target_pairs={{0,1},{1,2},{2,3},{3,0},{4,5},{5,6},{6,7},{7,4},{8,9},{9,10},{10,1... | collective-permute-start | bytes 98312 | tf_op jit(solution)/shard_map/ppermute | solution.py:20
  115.9 5.7 %collective-permute-start.2 = (bf16[8,2048]{1,0:T(8,128)(2,1)S(1)}, bf16[8,2048]{1,0:T(8,128)(2,1)S(1)}, u32[]{:S(2)}, u32[]{:S(2)}) collective-permute-start(bf16[8,2048]{1,0:T(8,128)(2,1)S(1)} %collective-permute-done.1), channel_id=1, source_target_pairs={{0,1},{1,2},{2,3},{3,0},{4,5},{5,6},{6,7},{7,4},{8,9},{9,10},{10,1... | collective-permute-start | bytes 98312 | tf_op jit(solution)/shard_map/ppermute | solution.py:20
  144.6 60.1 %reduce-scatter.8.cloned.1.call-start = ((), (), s32[]{:S(2)}) async-start(), calls=%async_computation.7 | async-start | bytes 163840 | tf_op jit(solution)/shard_map/reduce_scatter | solution.py:85
Sparse Core Ops, SparseCore 0:
  34.3 21.1 reduce-scatter.3
  86.5 16.7 reduce-scatter.5
  144.7 31.6 all-reduce.2
  185.3 19.4 reduce-scatter.7
